TPU v7x, 256 devices: a whole 4x4x8 slice. The times are simulated.
256 devices in a mesh: ctx: 64 (over y, z, core), kv: 4 (over x).
Axes of the slice: x: 4, y: 4, z: 8, core: 2. Of those that a mesh axis runs over, the one named last changes fastest.
Arguments:
- queries: bfloat16 [32768, 4, 2048], P('ctx', 'kv'), may hold values from -480 to 480
- keys: bfloat16 [32768, 4, 128], P('ctx', 'kv'), may hold values from -6 to 6
- values: bfloat16 [32768, 4, 128], P('ctx', 'kv'), may hold values from -6 to 6
- inputs: bfloat16 [32768, 4608], P('ctx', 'kv'), may hold values from -6 to 6
- gate_weight: bfloat16 [4608, 4, 32], P('kv'), may hold values from -0.09375 to 0.09375
- comp_one: bfloat16 [4, 2, 4096, 256], P('kv'), may hold values from -0.09375 to 0.09375
- comp_two: bfloat16 [4, 2, 256, 128], P('kv'), may hold values from -0.375 to 0.375
Outputs:
- attended: bfloat16 [32768, 4, 2048], P('ctx', 'kv')
All inputs are finite; a program needn't handle non-finite values.
Results may differ from a plain program's by a relative error of at most 0.0074.
Values may be sent and summed in bfloat16 or wider, within the bound.
A program may use at most 256 MiB of HBM per device.

v0:
```python
import math

import jax
import jax.numpy as jnp
from jax import lax
from jax.sharding import PartitionSpec as P

BLOCK = 32
STRIDE = 16
WINDOW = 512


def split_up(x, dim, count):
    before, after = (x.shape[:dim], x.shape[dim + 1 :])
    return jnp.moveaxis(x.reshape(*before, count, -1, *after), dim, 0)


def summed_on_arrival(x, axis, dim):
    pieces = split_up(x, dim, lax.axis_size(axis))
    arrived = lax.all_to_all(pieces, axis, split_axis=0, concat_axis=0, tiled=True)
    return arrived.astype(jnp.float32).sum(axis=0)


def from_behind(value, axis, steps):
    count = lax.axis_size(axis)
    first, last = (max(0, -steps), min(count, count - steps))
    return lax.ppermute(value, axis, [(source, source + steps) for source in range(first, last)])


def in_one_piece(arrays, axis, dim, along):
    ends, at = ([], 0)
    for a in arrays[:-1]:
        at += a.shape[along]
        ends.append(at)
    both = jnp.concatenate(arrays, axis=along)
    return tuple(jnp.split(lax.all_gather(both, axis, axis=dim, tiled=True), ends, axis=along))


def compress_local(blocks, comp_one, comp_two):
    groups = blocks.shape[3]
    head_dim = blocks.shape[4]
    weights = comp_one.reshape(groups, 2, BLOCK, head_dim, comp_one.shape[-1])
    hidden = jnp.einsum("snbgd,gsbde->sgne", blocks, weights, preferred_element_type=jnp.float32)
    hidden = jax.nn.gelu(hidden).astype(jnp.bfloat16)
    return jnp.einsum(
        "sgne,gsef->sngf", hidden, comp_two, preferred_element_type=jnp.float32
    ).astype(jnp.bfloat16)


def attend_far(state, key_piece, value_piece, first, query_all, token_pos, last_valid, scale):
    top, total, accum = state
    block_ids = first + jnp.arange(key_piece.shape[0], dtype=jnp.int32)
    visible = (
        (block_ids[None, :] >= 0)
        & (block_ids[None, :] <= last_valid)
        & (STRIDE * block_ids[None, :] + BLOCK - 1 <= token_pos[:, None])
    )
    scores = (
        jnp.einsum("tghd,jgd->tghj", query_all, key_piece, preferred_element_type=jnp.float32)
        * scale
    )
    scores = jnp.where(visible[:, None, None, :], scores, -jnp.inf)
    new_top = jnp.maximum(top, jnp.max(scores, axis=-1))
    factor = jnp.exp(top - new_top)
    expos = jnp.exp(scores - new_top[..., None])
    total = total * factor + jnp.sum(expos, axis=-1)
    accum = jnp.einsum(
        "tghj,jgd->tghd",
        expos.astype(jnp.bfloat16),
        value_piece,
        preferred_element_type=jnp.float32,
    )
    return (new_top, total, accum)


def window_part(query_all, key_ext, value_ext, my_start, scale):
    tok_count = query_all.shape[0]
    span = math.gcd(tok_count, 512)

    def one_block(number):
        offset = number * span
        token_pos = offset + jnp.arange(span, dtype=jnp.int32)
        key_pos = offset - WINDOW + jnp.arange(WINDOW + span, dtype=jnp.int32)
        visible = (
            (key_pos[None, :] > token_pos[:, None] - WINDOW)
            & (key_pos[None, :] <= token_pos[:, None])
            & (my_start + key_pos[None, :] >= 0)
        )
        scores = (
            jnp.einsum("tghd,jgd->tghj", query_all, key_ext, preferred_element_type=jnp.float32)
            * scale
        )
        scores = jnp.where(visible[:, None, None, :], scores, -jnp.inf)
        top = jnp.max(scores, axis=-1, keepdims=True)
        expos = jnp.exp(scores - top)
        total = jnp.sum(expos, axis=-1)
        summed = jnp.einsum(
            "tghj,jgd->tghd",
            expos.astype(jnp.bfloat16),
            value_ext,
            preferred_element_type=jnp.float32,
        )
        return summed / total[..., None]

    result = lax.map(one_block, jnp.arange(tok_count // span, dtype=jnp.int32))
    return result.reshape((tok_count,) + result.shape[2:])


def on_device(queries, keys, values, inputs, gate_weight, comp_one, comp_two):
    tok_count = queries.shape[0]
    groups = keys.shape[1]
    head_dim = keys.shape[2]
    heads = queries.shape[2] // head_dim
    scale = head_dim ** (-0.5)
    ctx_count = lax.axis_size("ctx")
    position = lax.axis_index("ctx")
    my_start = position * tok_count
    partial_value = jnp.dot(
        inputs, gate_weight.reshape(gate_weight.shape[0], -1), preferred_element_type=jnp.float32
    )
    partial_value = partial_value.reshape(tok_count, -1, 2 * heads)
    gate_logits = summed_on_arrival(partial_value.astype(jnp.bfloat16), "kv", 1)
    rim_keys, rim_values = from_behind((keys, values), "ctx", 1)
    per_device = tok_count // STRIDE
    stacked = jnp.stack(
        [
            jnp.concatenate([rim_keys[WINDOW - STRIDE :], keys]),
            jnp.concatenate([rim_values[WINDOW - STRIDE :], values]),
        ]
    )
    block_shift = -1
    pieces = stacked.reshape(2, per_device + 1, STRIDE, groups, head_dim)
    blocks = jnp.concatenate([pieces[:, :-1], pieces[:, 1:]], axis=2)
    packed = compress_local(blocks, comp_one, comp_two)
    query_all = queries.reshape(tok_count, groups, heads, head_dim)
    token_pos = my_start + jnp.arange(tok_count, dtype=jnp.int32)
    last_token = my_start + tok_count - 1
    last_valid = ctx_count * per_device - 2
    initial = (
        jnp.zeros((tok_count, groups, heads), jnp.float32),
        jnp.ones((tok_count, groups, heads), jnp.float32),
        jnp.zeros((tok_count, groups, heads, head_dim), jnp.float32),
    )
    piece = in_one_piece((packed[0], packed[1]), "ctx", 0, 1)
    key_piece = piece[0]
    value_piece = piece[1]
    first = jnp.int32(0) + block_shift
    needed = STRIDE * first + BLOCK - 1 <= last_token
    state = lax.cond(
        needed,
        lambda current: attend_far(
            current, key_piece, value_piece, first, query_all, token_pos, last_valid, scale
        ),
        lambda current: current,
        initial,
    )
    far = state[2] / state[1][..., None]
    key_ext = jnp.concatenate([rim_keys, keys])
    value_ext = jnp.concatenate([rim_values, values])
    near = window_part(query_all, key_ext, value_ext, my_start, scale)
    gates = jax.nn.sigmoid(gate_logits)
    mixed = gates[..., :heads, None] * far + gates[..., heads:, None] * near
    return mixed.reshape(tok_count, groups, heads * head_dim).astype(jnp.bfloat16)


def solution(mesh):
    placed = (
        P("ctx", "kv", None),
        P("ctx", "kv", None),
        P("ctx", "kv", None),
        P("ctx", "kv"),
        P("kv", None, None),
        P("kv", None, None, None),
        P("kv", None, None, None),
    )
    return jax.shard_map(
        on_device, mesh=mesh, in_specs=placed, out_specs=P("ctx", "kv", None), check_vma=False
    )
```

profile of v0, /device:TPU:24, one launch (start us, length us, event | category | flops | bytes accessed | tf_op | source)
XLA Modules:
  0.0 213.4 jit_solution(7694695076337428998)
XLA Ops:
  6.5 0.0 copy-start
  6.5 1.8 copy.35
  8.3 1.9 collective-permute-start.1
  10.2 3.9 %collective-permute-start = (bf16[512,1,128]{2,0,1:T(8,128)(2,1)}, bf16[512,1,128]{2,0,1:T(8,128)(2,1)S(1)}, u32[]{:S(2)}, u32[]{:S(2)}) collective-permute-start(bf16[512,1,128]{2,0,1:T(8,128)(2,1)} %param.10), channel_id=1, source_target_pairs={{0,4},{4,8},{8,12},{12,16},{16,20},{20,24},{24,28},{28,32},{32,36}... | collective-permute-start | bytes 393224 | tf_op jit(solution)/shard_map/ppermute | solution.py:27
  14.1 0.0 copy-done
  14.2 2.1 fusion.40
  16.3 4.3 %all-to-all-start = ((bf16[4,512,1,32]{1,3,2,0:T(8,128)(2,1)}), bf16[4,512,1,32]{1,3,2,0:T(8,128)(2,1)S(1)}, u32[]{:S(2)}, u32[]{:S(2)}) async-start(bf16[4,512,1,32]{1,3,2,0:T(8,128)(2,1)} %fusion.40), calls=%async_computation | async-start | bytes 262144 | tf_op jit(solution)/shard_map/all_to_all | solution.py:20
  20.6 0.0 all-gather.2.cloned.1.call-start
  20.6 1.6 fusion.34
  22.2 2.2 %copy.52 = bf16[64,8,16,128]{3,2,1,0:T(8,128)(2,1)S(1)} copy(bf16[64,8,16,128]{3,1,2,0:T(8,128)(2,1)} %bitcast.151) | data formatting | bytes 4194304
  24.4 2.2 %all-to-all-done = bf16[4,512,1,32]{1,3,2,0:T(8,128)(2,1)S(1)} async-done(((bf16[4,512,1,32]{1,3,2,0:T(8,128)(2,1)}), bf16[4,512,1,32]{1,3,2,0:T(8,128)(2,1)S(1)}, u32[]{:S(2)}, u32[]{:S(2)}) %all-to-all-start) | async-done | bytes 131104 | tf_op jit(solution)/shard_map/all_to_all | solution.py:20
  26.6 0.6 slice_bitcast_fusion.1
  27.2 0.0 collective-permute-done.1
  27.2 0.8 slice.34
  28.1 0.1 copy.36
  28.1 0.9 pad_maximum_fusion.1
  29.1 0.0 collective-permute-done
  29.1 0.0 copy-start.3
  29.1 1.0 pad_maximum_fusion
  30.1 0.0 copy-done.3
  30.1 0.1 copy_dynamic-update-slice_fusion
  30.2 0.8 fusion.73
  31.0 3.2 %convolution_convert_fusion = bf16[2,32,128]{2,1,0:T(8,128)(2,1)S(1)} fusion(bf16[1,2,256,128]{3,2,1,0:T(8,128)(2,1)} %param.15, bf16[2,32,128,256]{3,2,1,0:T(8,128)(2,1)} %bitcast.152, bf16[2,32,16,1,128]{4,1,2,0,3:T(8,128)(2,1)} %get-tuple-element.61, bf16[2,32,16,1,128]{4,1,2,0,3:T(8,128)(2,1)S(1)} %get-tuple-element.60), kind=kOutput, calls=%fused_computation.47 | convolution fusion | flops 138829824 | bytes 4866048 | tf_op jit(solution)/shard_map/sgne,gsef->sngf/dot_general | solution.py:45
  34.3 0.6 pad_maximum_fusion.2
  34.9 0.0 all-gather.2.cloned.1.call-update
  34.9 0.0 copy-start.1
  34.9 14.6 %fusion.22 = (f32[512,16]{0,1:T(8,128)S(1)}, f32[1024,512,16]{1,0,2:T(8,128)}) fusion(pred[512,1024]{0,1:T(8,128)(4,1)} %fusion.34, bf16[512,16,128]{2,1,0:T(8,128)(2,1)S(1)} %bitcast.149, bf16[512,1,128]{2,0,1:T(8,128)(2,1)} %param.10, bf16[512,1,128]{2,0,1:T(8,128)(2,1)} %copy-done.3), kind=kOutput, calls=%fused_computation.29 | convolution fusion | flops 2173165568 | bytes 36470784 | tf_op jit(solution)/shard_map/while/body/eval_jaxpr/tghd,jgd->tghj/dot_general | solution.py:90
  49.5 0.0 copy-done.1
  49.6 14.4 %fusion.20 = f32[512,16]{0,1:T(8,128)S(1)} fusion(f32[1024,512,16]{1,0,2:T(8,128)} %get-tuple-element.65, f32[512,16]{0,1:T(8,128)S(1)} %get-tuple-element.64, pred[512,1024]{0,1:T(8,128)(4,1)S(1)} %copy-done.1), kind=kLoop, calls=%fused_computation.27 | loop fusion | flops 33546240 | bytes 34144256 | tf_op jit(solution)/shard_map/while/body/eval_jaxpr/reduce_sum | solution.py:96
  64.0 41.4 %all-gather.2.cloned.1.call-done = bf16[2048,2,128]{2,0,1:T(8,128)(2,1)} async-done(((bf16[32,2,128]{2,0,1:T(8,128)(2,1)}), bf16[2048,2,128]{2,0,1:T(8,128)(2,1)}) %all-gather.2.cloned.1.call-update) | async-done | bytes 1048592 | tf_op jit(solution)/shard_map/all_gather | solution.py:36
  105.3 0.0 copy-start.2
  105.3 0.0 copy-start.4
  105.3 0.0 copy-start.5
  105.3 80.0 %conditional.1 = (f32[512,1,16]{0,2,1:T(8,128)S(1)}, f32[512,1,16,128]{0,3,2,1:T(8,128)}) conditional(s32[]{:T(128)} %convert_element_type.48, () %tuple.15, (s32[]{:T(128)}, s32[512]{0:T(512)S(1)}, bf16[2048,2,128]{2,0,1:T(8,128)(2,1)}, bf16[512,1,2048]{2,0,1:T(8,128)(2,1)}) %tuple.16), branch_computations={%region_1.0_spmd, %region_2.5_spmd} | conditional | flops 8776611840 | bytes 217376784 | solution.py:149
  105.4 1.5 compare_and_fusion
  106.9 3.9 %copy.40 = bf16[512,1,2048]{0,2,1:T(8,128)(2,1)} copy(bf16[512,1,2048]{2,0,1:T(8,128)(2,1)} %get-tuple-element.56) | data formatting | bytes 4194304 | tf_op jit(solution)/shard_map
  110.8 26.0 %fusion.2 = (f32[512,16]{0,1:T(8,128)S(1)}, f32[2048,512,16]{1,0,2:T(8,128)}) fusion(pred[512,2048]{0,1:T(8,128)(4,1)S(1)} %compare_and_fusion, bf16[512,16,128]{0,2,1:T(8,128)(2,1)} %bitcast.150, bf16[2048,2,128]{2,0,1:T(8,128)(2,1)} %get-tuple-element.39), kind=kOutput, calls=%fused_computation.4 | convolution fusion | flops 4345290752 | bytes 70811648 | tf_op jit(solution)/shard_map/cond/branch_1_fun/tghd,jgd->tghj/dot_general | solution.py:59
  136.8 21.5 %fusion.1 = f32[512,16]{0,1:T(8,128)S(1)} fusion(f32[2048,512,16]{1,0,2:T(8,128)} %get-tuple-element.59, f32[512,16]{0,1:T(8,128)S(1)} %broadcast_maximum_fusion, pred[512,2048]{0,1:T(8,128)(4,1)S(1)} %compare_and_fusion), kind=kLoop, calls=%fused_computation.3 | loop fusion | flops 67100672 | bytes 68222976 | tf_op jit(solution)/shard_map/cond/branch_1_fun/reduce_sum | solution.py:66
  158.4 26.9 %fusion.7 = f32[512,1,16,128]{0,3,2,1:T(8,128)} fusion(f32[2048,512,16]{1,0,2:T(8,128)} %get-tuple-element.59, f32[512,16]{0,1:T(8,128)S(1)} %broadcast_maximum_fusion, pred[512,2048]{0,1:T(8,128)(4,1)S(1)} %compare_and_fusion, bf16[2048,2,128]{2,0,1:T(8,128)(2,1)} %get-tuple-element.39), kind=kOutput, calls=%fused_computation.9 | convolution fusion | flops 4362076160 | bytes 72908800 | tf_op jit(solution)/shard_map/cond/branch_1_fun/tghj,jgd->tghd/dot_general | solution.py:67
  185.3 0.0 copy-done.2
  185.3 0.0 copy-done.4
  185.3 0.0 copy-done.5
  185.3 17.3 %fusion.27 = bf16[512,1,16,128]{0,3,2,1:T(8,128)(2,1)} fusion(f32[512,1,16,128]{0,3,2,1:T(8,128)} %get-tuple-element.57, f32[1024,512,16]{1,0,2:T(8,128)} %get-tuple-element.65, f32[512,16]{0,1:T(8,128)S(1)} %get-tuple-element.64, pred[512,1024]{0,1:T(8,128)(4,1)S(1)} %copy-done.2, f32[512,16]{0,1:T(8,128)S(1)} %fusion.20, f32[512,16]{0,1:T(8,128)S(1)} %copy-done.5, ...), kind=kOutput, calls=%fused_computation.34 | convolution fusion | flops 2187853824 | bytes 40796160 | tf_op jit(solution)/shard_map/while/body/eval_jaxpr/tghj,jgd->tghd/dot_general | solution.py:97
  202.6 3.9 %copy.45 = bf16[512,1,2048]{2,0,1:T(8,128)(2,1)} copy(bf16[512,1,2048]{0,2,1:T(8,128)(2,1)} %bitcast.153) | data formatting | bytes 4194304 | tf_op jit(solution)/shard_map/convert_element_type | solution.py:163
  (15 shorter events, 0.2 us)
Async XLA Ops:
  6.5 7.6 %copy-start = (bf16[512,1152]{1,0:T(8,128)(2,1)S(1)}, bf16[512,1152]{1,0:T(8,128)(2,1)}, u32[]{:S(2)}) copy-start(bf16[512,1152]{1,0:T(8,128)(2,1)} %param.12) | copy-start | bytes 3538948
  8.3 19.0 %collective-permute-start.1 = (bf16[512,1,128]{0,2,1:T(8,128)(2,1)}, bf16[512,1,128]{0,2,1:T(8,128)(2,1)}, u32[]{:S(2)}, u32[]{:S(2)}) collective-permute-start(bf16[512,1,128]{0,2,1:T(8,128)(2,1)} %copy.35), channel_id=1, source_target_pairs={{0,4},{4,8},{8,12},{12,16},{16,20},{20,24},{24,28},{28,32},{32,36}... | collective-permute-start | bytes 393224 | tf_op jit(solution)/shard_map/ppermute | solution.py:27
  10.2 18.9 %collective-permute-start = (bf16[512,1,128]{2,0,1:T(8,128)(2,1)}, bf16[512,1,128]{2,0,1:T(8,128)(2,1)S(1)}, u32[]{:S(2)}, u32[]{:S(2)}) collective-permute-start(bf16[512,1,128]{2,0,1:T(8,128)(2,1)} %param.10), channel_id=1, source_target_pairs={{0,4},{4,8},{8,12},{12,16},{16,20},{20,24},{24,28},{28,32},{32,36}... | collective-permute-start | bytes 393224 | tf_op jit(solution)/shard_map/ppermute | solution.py:27
  16.3 10.3 %all-to-all-start = ((bf16[4,512,1,32]{1,3,2,0:T(8,128)(2,1)}), bf16[4,512,1,32]{1,3,2,0:T(8,128)(2,1)S(1)}, u32[]{:S(2)}, u32[]{:S(2)}) async-start(bf16[4,512,1,32]{1,3,2,0:T(8,128)(2,1)} %fusion.40), calls=%async_computation | async-start | bytes 262144 | tf_op jit(solution)/shard_map/all_to_all | solution.py:20
  20.6 84.7 %all-gather.2.cloned.1.call-start = ((), (), s32[]{:S(2)}) async-start(), calls=%async_computation.1 | async-start | bytes 1064960 | tf_op jit(solution)/shard_map/all_gather | solution.py:36
  29.1 1.0 copy-start.3
  34.9 14.6 %copy-start.1 = (pred[512,1024]{0,1:T(8,128)(4,1)S(1)}, pred[512,1024]{0,1:T(8,128)(4,1)}, u32[]{:S(2)}) copy-start(pred[512,1024]{0,1:T(8,128)(4,1)} %fusion.34) | copy-start | bytes 1572868
  105.3 80.0 %copy-start.2 = (pred[512,1024]{0,1:T(8,128)(4,1)S(1)}, pred[512,1024]{0,1:T(8,128)(4,1)}, u32[]{:S(2)}) copy-start(pred[512,1024]{0,1:T(8,128)(4,1)} %fusion.34) | copy-start | bytes 1572868
  105.3 80.0 %copy-start.4 = (f32[512,16]{0,1:T(8,128)S(1)}, f32[512,16]{0,1:T(8,128)}, u32[]{:S(2)}) copy-start(f32[512,16]{0,1:T(8,128)} %get-tuple-element.62) | copy-start | bytes 98308
  105.3 80.0 %copy-start.5 = (f32[512,16]{0,1:T(8,128)S(1)}, f32[512,16]{0,1:T(8,128)}, u32[]{:S(2)}) copy-start(f32[512,16]{0,1:T(8,128)} %get-tuple-element.63) | copy-start | bytes 98308
Sparse Core Ops, SparseCore 0:
  35.1 70.2 all-gather.1
where the time goes:
time: 216 us; the launch traced here: 213 us
  matrix products  90.2 us (42%)
  waiting for transfers between devices  43.6 us (20%)
  other arithmetic  41.6 us (19%)
  local copies, waits for them, and re-layouts  14.3 us (7%)
  between operations  13.5 us (6%)
  starting transfers between devices  10.1 us (5%)
    all_gather x1, waiting for transfers between devices, in_one_piece(): lax.all_gather(both, axis, axis=dim, tiled=True)  41.4 us
    dot_general x1, matrix products, attend_far(): jnp.einsum('tghj,jgd->tghd', expos.astype(jnp.bfloat16), value_piece, pre...  26.9 us
    dot_general x1, matrix products, attend_far(): jnp.einsum('tghd,jgd->tghj', query_all, key_piece, preferred_element_type...  26 us
    reduce_sum x1, other arithmetic, attend_far(): total = total * factor + jnp.sum(expos, axis=-1)  21.5 us
    dot_general x1, matrix products, one_block(): jnp.einsum('tghj,jgd->tghd', expos.astype(jnp.bfloat16), value_ext, prefe...  17.3 us
    dot_general x1, matrix products, one_block(): jnp.einsum('tghd,jgd->tghj', query_all, key_ext, preferred_element_type=j...  14.6 us
    reduce_sum x1, other arithmetic, one_block(): total = jnp.sum(expos, axis=-1)  14.4 us
    ppermute x2, starting transfers between devices, from_behind(): lax.ppermute(value, axis, [(source, source + steps) for source in range(f...  5.84 us
  transfers between devices with their start and end apart: 4, of which 2 were waited for; matrix products, arithmetic and copies ran while one was open for 18% of the time, Pallas kernels for 0%

commit v1 on v0

v1 whole, which is shorter than its diff:
```python
import functools

import jax
import jax.numpy as jnp
from jax import lax
from jax.experimental import pallas as pl
from jax.experimental.pallas import tpu as pltpu
from jax.sharding import PartitionSpec as P

MESH = pl.DeviceIdType.MESH
F32 = jnp.float32
BF16 = jnp.bfloat16
BLOCK = 32
STRIDE = 16
WINDOW = 512
NEG = -1e30
LOG2E = 1.4426950408889634
NT = (((1,), (1,)), ((), ()))
KC = 512
HALF = 256


def kernel(
    dims,
    q_hbm, keys_hbm, values_hbm, inputs_hbm, gate_w_hbm, one_hbm, two_hbm,
    out_hbm,
    q_v, out_v, inp_v, gw_v, one_v, two_v,
    wk, wv, rim, kv_f32, wvt, gath, cvt, gate_send, gate_recv, gates,
    s0, s1, c0, c1, m_ref, acc_ref, near_ref, far_bias, near_bias,
    in_sem, out_sem, rim_sem, win_sem, gate_sem, y1_sem, z1_sem, z2_sem, y2_sem, core_sem,
):
    ny, nz, nc, nkv, heads = dims
    n_ctx = ny * nz * nc
    me = lax.axis_index("ctx")
    group = lax.axis_index("kv")
    y, z, core = me // (nz * nc), (me // nc) % nz, me % nc
    tok = q_v.shape[0]
    hd = wk.shape[1]
    scale = hd ** -0.5 * LOG2E
    right, left = lax.rem(me + 1, n_ctx), lax.rem(me + n_ctx - 1, n_ctx)

    def ctx_of(yy, zz, cc):
        return (yy * nz + zz) * nc + cc

    y_peer = lambda d: ctx_of(lax.rem(y + d, ny), z, core)
    z_peer = lambda d: ctx_of(y, lax.rem(z + d, nz), core)
    partner = ctx_of(y, z, 1 - core)
    kv_peer = lambda d: lax.rem(group + d, nkv)

    def load(src, dst, n):
        return pltpu.make_async_copy(src, dst, in_sem.at[n])

    loads = [
        load(keys_hbm, wk.at[pl.ds(WINDOW, tok), :], 0),
        load(values_hbm, wv.at[pl.ds(WINDOW, tok), :], 1),
        load(inputs_hbm, inp_v, 2),
        load(gate_w_hbm, gw_v, 3),
        load(one_hbm.at[0], one_v.at[0], 4),
        load(one_hbm.at[1], one_v.at[1], 5),
        load(two_hbm, two_v, 6),
        load(q_hbm, q_v, 7),
    ]
    for c in loads:
        c.start()

    barrier = pltpu.get_barrier_semaphore()
    n_sig = 0
    for d in range(1, ny):
        pl.semaphore_signal(barrier, inc=1, device_id={"ctx": y_peer(d)}, device_id_type=MESH)
        n_sig += 1
    for d in range(1, nz):
        pl.semaphore_signal(barrier, inc=1, device_id={"ctx": z_peer(d)}, device_id_type=MESH)
        n_sig += 1
    for other in (partner, left, right):
        pl.semaphore_signal(barrier, inc=1, device_id={"ctx": other}, device_id_type=MESH)
        n_sig += 1
    for d in range(1, nkv):
        pl.semaphore_signal(barrier, inc=1, device_id={"kv": kv_peer(d)}, device_id_type=MESH)
        n_sig += 1

    loads[2].wait()
    loads[3].wait()
    part = lax.dot_general(gw_v[...], inp_v[...], NT, preferred_element_type=F32)
    gate_send[...] = part.astype(BF16).reshape(gate_send.shape)
    loads[0].wait()
    loads[1].wait()

    pl.semaphore_wait(barrier, n_sig)

    def remote(src, dst, sems, n, **where):
        return pltpu.make_async_remote_copy(
            src_ref=src, dst_ref=dst, send_sem=sems.at[0, n], recv_sem=sems.at[1, n],
            device_id=where, device_id_type=MESH,
        )

    tail = pl.ds(WINDOW + tok - STRIDE, STRIDE)
    rim_k = remote(wk.at[tail, :], rim.at[0], rim_sem, 0, ctx=right)
    rim_v = remote(wv.at[tail, :], rim.at[1], rim_sem, 1, ctx=right)
    rim_k.start()
    rim_v.start()
    gate_copies = []
    for d in range(1, nkv):
        to = kv_peer(d)
        gate_copies.append(remote(gate_send.at[to], gate_recv.at[d], gate_sem, d, kv=to))
        gate_copies[-1].start()
    win_k = remote(wk.at[pl.ds(tok, WINDOW), :], wk.at[pl.ds(0, WINDOW), :], win_sem, 0, ctx=right)
    win_v = remote(wv.at[pl.ds(tok, WINDOW), :], wv.at[pl.ds(0, WINDOW), :], win_sem, 1, ctx=right)
    win_k.start()
    win_v.start()

    kv_f32[0, pl.ds(STRIDE, tok), :] = wk[pl.ds(WINDOW, tok), :].astype(F32)
    kv_f32[1, pl.ds(STRIDE, tok), :] = wv[pl.ds(WINDOW, tok), :].astype(F32)
    rim_k.wait()
    rim_v.wait()
    kv_f32[0, :STRIDE, :] = rim[0].astype(F32)
    kv_f32[1, :STRIDE, :] = rim[1].astype(F32)
    loads[6].wait()
    nb = tok // STRIDE
    row = lax.broadcasted_iota(jnp.int32, (nb, hd), 0)
    for s in range(2):
        flat = jnp.concatenate(
            [kv_f32[s, pl.ds(b, nb, stride=STRIDE), :] for b in range(BLOCK)], axis=1
        ).astype(BF16)
        loads[4 + s].wait()
        hidden = jnp.dot(flat, one_v[s], preferred_element_type=F32)
        hidden = jax.nn.gelu(hidden).astype(BF16)
        packed = jnp.dot(hidden, two_v[s], preferred_element_type=F32)
        packed = jnp.where((row == 0) & (me == 0), 0.0, packed)
        gath[s, y, z, core] = packed.astype(BF16)

    k1 = [remote(gath.at[0, y, z, core], gath.at[0, y, z, core], y1_sem, d, ctx=y_peer(d)) for d in range(1, ny)]
    v1 = [remote(gath.at[1, y, z, core], gath.at[1, y, z, core], z1_sem, d, ctx=z_peer(d)) for d in range(1, nz)]
    for c in k1 + v1:
        c.start()

    nfull = (me * nb) // KC
    ids = lax.broadcasted_iota(jnp.int32, (KC, tok), 0) + nfull * KC
    at = lax.broadcasted_iota(jnp.int32, (KC, tok), 1) + tok * me
    far_bias[...] = jnp.where((ids * STRIDE + STRIDE - 1 <= at) | (ids == 0), 0.0, NEG)
    width = WINDOW + HALF
    for i in range(tok // HALF):
        w = lax.broadcasted_iota(jnp.int32, (width, HALF), 0)
        t = lax.broadcasted_iota(jnp.int32, (width, HALF), 1)
        low = jnp.where(me == 0, WINDOW - i * HALF, 0)
        near_bias[:, i * HALF : (i + 1) * HALF] = jnp.where(
            (w > t) & (w <= t + WINDOW) & (w >= low), 0.0, NEG
        )
    extra = wvt.shape[0] - hd
    one_row = lambda n: jnp.where(
        lax.broadcasted_iota(jnp.int32, (extra, n), 0) == 0, 1.0, 0.0
    ).astype(BF16)
    wvt[hd:, :] = one_row(WINDOW + tok)
    cvt[hd:, :] = one_row(cvt.shape[1])
    wvt[:hd, WINDOW:] = kv_f32[1, pl.ds(STRIDE, tok), :].T.astype(BF16)

    logits = gate_send[group].astype(F32)
    for d in range(1, nkv):
        gate_copies[d - 1].wait()
        logits = logits + gate_recv[d].astype(F32)
    gates[...] = jax.nn.sigmoid(logits)

    win_k.wait()
    win_v.wait()
    wvt[:hd, :WINDOW] = wv[:WINDOW, :].astype(F32).T.astype(BF16)
    loads[7].wait()

    k2 = [remote(gath.at[0, :, z, core], gath.at[0, :, z, core], z2_sem, d, ctx=z_peer(d)) for d in range(1, nz)]
    v2 = [remote(gath.at[1, y, :, core], gath.at[1, y, :, core], y2_sem, d, ctx=y_peer(d)) for d in range(1, ny)]
    swap = remote(gath.at[:, :, :, core], gath.at[:, :, :, core], core_sem, 0, ctx=partner)

    def second():
        for c in k1 + v1:
            c.wait()
        for c in k2 + v2:
            c.start()

    def third():
        for c in k2 + v2:
            c.wait()
        swap.start()

    def head_cols(h):
        return pl.ds(pl.multiple_of(h * hd, hd), hd)

    def fold(s):
        return jnp.max(s.reshape(s.shape[0] // 8, 8, s.shape[1]), axis=0)

    def near_scores(h, s_ref, c_ref):
        for i in range(tok // HALF):
            cols = slice(i * HALF, (i + 1) * HALF)
            s = lax.dot_general(
                wk[i * HALF : i * HALF + width, :], q_v[cols, head_cols(h)], NT,
                preferred_element_type=F32,
            )
            s = s + near_bias[:, cols]
            s_ref[:, cols] = s
            c_ref[:, cols] = fold(s)

    def near_values(h, s_ref, c_ref):
        m = jnp.max(c_ref[...], axis=0, keepdims=True) * scale
        e = jnp.exp2(s_ref[...] * scale - m).astype(BF16)
        for i in range(tok // HALF):
            cols = slice(i * HALF, (i + 1) * HALF)
            o = jnp.dot(wvt[:, i * HALF : i * HALF + width], e[:, cols], preferred_element_type=F32)
            near_ref[h, :, cols] = o[:hd] * (gates[pl.ds(heads + h, 1), cols] / o[hd : hd + 1])

    near_scores(0, s0, c0)

    def near_pair(j, carry):
        h = 2 * j
        near_scores(h + 1, s1, c1)
        near_values(h, s0, c0)
        near_scores(jnp.minimum(h + 2, heads - 2), s0, c0)
        near_values(h + 1, s1, c1)
        pl.when(j == STEP2)(second)
        pl.when(j == STEP3)(third)
        return carry

    lax.fori_loop(0, heads // 2, near_pair, 0)

    swap.wait()
    per_y = nz * nc * nb
    for i in range(ny):
        vals = gath[1, i].reshape(per_y, hd)
        cvt[:hd, i * per_y : (i + 1) * per_y] = vals.astype(F32).T.astype(BF16)

    m_ref[...] = jnp.zeros_like(m_ref)
    acc_ref[...] = jnp.zeros_like(acc_ref)

    def far_scores(c, h, s_ref, c_ref, masked):
        k = gath[0, c].reshape(KC, hd)
        s = lax.dot_general(k, q_v[:, head_cols(h)], NT, preferred_element_type=F32)
        if masked:
            s = s + far_bias[...]
        s_ref[:KC, :] = s
        c_ref[...] = fold(s)

    def far_values(c, h, s_ref, c_ref):
        m_old = m_ref[pl.ds(h, 1), :]
        m = jnp.maximum(jnp.max(c_ref[...], axis=0, keepdims=True) * scale, m_old)
        e = jnp.exp2(s_ref[:KC, :] * scale - m).astype(BF16)
        vt = cvt[:, pl.ds(pl.multiple_of(c * KC, KC), KC)]
        o = jnp.dot(vt, e, preferred_element_type=F32)
        acc_ref[h] = acc_ref[h] * jnp.exp2(m_old - m) + o
        m_ref[pl.ds(h, 1), :] = m

    def far_sweep(chunk_of, head_of, count, masked):
        far_scores(chunk_of(0), head_of(0), s0, c0, masked)

        def pair(j, carry):
            n = 2 * j
            far_scores(chunk_of(n + 1), head_of(n + 1), s1, c1, masked)
            far_values(chunk_of(n), head_of(n), s0, c0)
            nxt = jnp.minimum(n + 2, count - 2)
            far_scores(chunk_of(nxt), head_of(nxt), s0, c0, masked)
            far_values(chunk_of(n + 1), head_of(n + 1), s1, c1)
            return carry

        lax.fori_loop(0, count // 2, pair, 0)

    @pl.when(nfull > 0)
    def _():
        far_sweep(lambda n: n // heads, lambda n: lax.rem(n, heads), nfull * heads, False)

    far_sweep(lambda n: nfull, lambda n: n, heads, True)

    def put(h):
        return pltpu.make_async_copy(out_v.at[:, head_cols(h)], out_hbm.at[:, head_cols(h)], out_sem.at[h])

    def finish(h, carry):
        o = acc_ref[h]
        r = o[:hd] * (gates[pl.ds(h, 1), :] / o[hd : hd + 1]) + near_ref[h]
        out_v[:, head_cols(h)] = r.T.astype(BF16)
        put(h).start()
        return carry

    lax.fori_loop(0, heads, finish, 0)
    for h in range(heads):
        put(h).wait()


STEP2, STEP3 = 2, 6


def on_device(dims, queries, keys, values, inputs, gate_weight, comp_one, comp_two):
    ny, nz, nc, nkv, heads = dims
    tok = queries.shape[0]
    hd = keys.shape[2]
    depth = inputs.shape[1]
    hid = comp_one.shape[3]
    gate_rows = gate_weight.shape[1] * gate_weight.shape[2]
    cols = ny * nz * nc * (tok // STRIDE)
    q = queries.reshape(tok, heads * hd)
    gate_w = gate_weight.transpose(1, 2, 0).reshape(gate_rows, depth)
    any_spec = pl.BlockSpec(memory_space=pl.ANY)
    vm = pltpu.VMEM
    dma = pltpu.SemaphoreType.DMA
    width = WINDOW + HALF
    out = pl.pallas_call(
        functools.partial(kernel, dims),
        out_shape=jax.ShapeDtypeStruct((tok, heads * hd), BF16),
        in_specs=[any_spec] * 7,
        out_specs=any_spec,
        scratch_shapes=[
            vm((tok, heads * hd), BF16),
            vm((tok, heads * hd), BF16),
            vm((tok, depth), BF16),
            vm((gate_rows, depth), BF16),
            vm((2, BLOCK * hd, hid), BF16),
            vm((2, hid, hd), BF16),
            vm((WINDOW + tok, hd), BF16),
            vm((WINDOW + tok, hd), BF16),
            vm((2, STRIDE, hd), BF16),
            vm((2, STRIDE + tok, hd), F32),
            vm((hd + 16, WINDOW + tok), BF16),
            vm((2, ny, nz, nc, tok // STRIDE, hd), BF16),
            vm((hd + 16, cols), BF16),
            vm((nkv, 2 * heads, tok), BF16),
            vm((nkv, 2 * heads, tok), BF16),
            vm((2 * heads, tok), F32),
            vm((width, tok), F32),
            vm((width, tok), F32),
            vm((8, tok), F32),
            vm((8, tok), F32),
            vm((heads, tok), F32),
            vm((heads, hd + 16, tok), F32),
            vm((heads, hd, tok), F32),
            vm((KC, tok), F32),
            vm((width, tok), F32),
            dma((8,)),
            dma((heads,)),
            dma((2, 2)),
            dma((2, 2)),
            dma((2, nkv)),
            dma((2, ny)),
            dma((2, nz)),
            dma((2, nz)),
            dma((2, ny)),
            dma((2, 1)),
        ],
        compiler_params=pltpu.CompilerParams(
            collective_id=0, has_side_effects=True, vmem_limit_bytes=58 * 1024 * 1024
        ),
        name="attend",
    )(
        q,
        keys.reshape(tok, hd),
        values.reshape(tok, hd),
        inputs,
        gate_w,
        comp_one.reshape(comp_one.shape[1:]),
        comp_two.reshape(comp_two.shape[1:]),
    )
    return out.reshape(tok, 1, heads * hd)


def solution(mesh):
    placed = (
        P("ctx", "kv", None),
        P("ctx", "kv", None),
        P("ctx", "kv", None),
        P("ctx", "kv"),
        P("kv", None, None),
        P("kv", None, None, None),
        P("kv", None, None, None),
    )
    dims = (4, mesh.shape["ctx"] // 8, 2, mesh.shape["kv"], 16)
    return jax.shard_map(
        functools.partial(on_device, dims),
        mesh=mesh, in_specs=placed, out_specs=P("ctx", "kv", None), check_vma=False,
    )
```

time: 216 us -> 56.3 us (0.26)
  matrix products: 90.2 us -> 0 us
  Pallas kernels: 0 us -> 52.5 us
  waiting for transfers between devices: 43.6 us -> 0 us
  other arithmetic: 41.6 us -> 0 us
  between operations: 13.5 us -> 0.01 us
  local copies, waits for them, and re-layouts: 14.3 us -> 3.16 us
  starting transfers between devices: 10.1 us -> 0 us
    dot_general x6 -> x0, matrix products: 90.2 us -> none  [the longest x1 26.9 us: attend_far(): jnp.einsum('tghj,jgd->tghd', expos.astype(jnp.bfloat16), value_piece, pre...]
    pallas_call x0 -> x1, Pallas kernels: none -> 52.5 us  [on_device(): pl.pallas_call(functools.partial(kernel, dims), out_shape=jax.ShapeDtypeS...]
    all_gather x1 -> x0, waiting for transfers between devices: 41.4 us -> none  [in_one_piece(): lax.all_gather(both, axis, axis=dim, tiled=True)]
    reduce_sum x3 -> x0, other arithmetic: 36 us -> none  [the longest x1 21.5 us: attend_far(): total = total * factor + jnp.sum(expos, axis=-1)]
    ppermute x2 -> x0, starting transfers between devices: 5.84 us -> none  [from_behind(): lax.ppermute(value, axis, [(source, source + steps) for source in range(f...]
    all_to_all x1 -> x0, starting transfers between devices: 4.3 us -> none  [summed_on_arrival(): lax.all_to_all(pieces, axis, split_axis=0, concat_axis=0, tiled=True)]
    another operation x2 -> x0, local copies, waits for them, and re-layouts: 3.99 us -> none
    convert_element_type x1 -> x0, local copies, waits for them, and re-layouts: 3.91 us -> none  [on_device(): mixed.reshape(tok_count, groups, heads * head_dim).astype(jnp.bfloat16)]
  transfers between devices with their start and end apart: 4 -> 0, of which waited for: 2 -> 0; matrix products, arithmetic and copies ran while one was open for 18% -> 0% of each run, Pallas kernels for 0% -> 0%
where the time goes in v1:
time: 56.3 us; the launch traced here: 55.7 us
  Pallas kernels  52.5 us (93%)
  local copies, waits for them, and re-layouts  3.16 us (6%)
    pallas_call x1, Pallas kernels, on_device(): pl.pallas_call(functools.partial(kernel, dims), out_shape=jax.ShapeDtypeS...  52.5 us
    unnamed x1, local copies, waits for them, and re-layouts  3.16 us

profile of v1, /device:TPU:24, one launch (start us, length us, event | category | flops | bytes accessed | tf_op | source)
XLA Modules:
  0.0 55.7 jit_solution(16881867307235127734)
XLA Ops:
  0.0 52.5 %attend.1 = bf16[512,2048]{1,0:T(8,128)(2,1)} custom-call(bf16[512,2048]{1,0:T(8,128)(2,1)} %bitcast.11, bf16[512,128]{1,0:T(8,128)(2,1)} %bitcast.13, bf16[512,128]{1,0:T(8,128)(2,1)} %bitcast.14, bf16[512,1152]{1,0:T(8,128)(2,1)} %inputs_hbm.1, bf16[128,1152]{1,0:T(8,128)(2,1)} %bitcast.12, bf16[2,4096,256]{2,1,0:T(8,128)(2,1)} %bitcast.10, ...), custom_call_target="tpu_custom_call" | custom-call | tf_op jit(solution)/shard_map/attend/pallas_call | solution.py:299
  52.5 3.2 %copy.9 = bf16[512,1,2048]{2,0,1:T(8,128)(2,1)} copy(bf16[512,1,2048]{2,0,1:T(8,128)(2,1)} %bitcast.9) | data formatting | bytes 4194304

commit v2 on v1

--- a/solution.py
+++ b/solution.py
@@ -53,12 +53,12 @@
     loads = [
         load(keys_hbm, wk.at[pl.ds(WINDOW, tok), :], 0),
         load(values_hbm, wv.at[pl.ds(WINDOW, tok), :], 1),
-        load(inputs_hbm, inp_v, 2),
-        load(gate_w_hbm, gw_v, 3),
-        load(one_hbm.at[0], one_v.at[0], 4),
-        load(one_hbm.at[1], one_v.at[1], 5),
-        load(two_hbm, two_v, 6),
+        load(one_hbm.at[0], one_v.at[0], 2),
+        load(one_hbm.at[1], one_v.at[1], 3),
+        load(two_hbm, two_v, 4),
         load(q_hbm, q_v, 7),
+        load(inputs_hbm, inp_v, 5),
+        load(gate_w_hbm, gw_v, 6),
     ]
     for c in loads:
         c.start()
@@ -78,12 +78,10 @@
         pl.semaphore_signal(barrier, inc=1, device_id={"kv": kv_peer(d)}, device_id_type=MESH)
         n_sig += 1
 
-    loads[2].wait()
-    loads[3].wait()
-    part = lax.dot_general(gw_v[...], inp_v[...], NT, preferred_element_type=F32)
-    gate_send[...] = part.astype(BF16).reshape(gate_send.shape)
     loads[0].wait()
     loads[1].wait()
+    kv_f32[0, pl.ds(STRIDE, tok), :] = wk[pl.ds(WINDOW, tok), :].astype(F32)
+    kv_f32[1, pl.ds(STRIDE, tok), :] = wv[pl.ds(WINDOW, tok), :].astype(F32)
 
     pl.semaphore_wait(barrier, n_sig)
 
@@ -98,45 +96,46 @@
     rim_v = remote(wv.at[tail, :], rim.at[1], rim_sem, 1, ctx=right)
     rim_k.start()
     rim_v.start()
-    gate_copies = []
-    for d in range(1, nkv):
-        to = kv_peer(d)
-        gate_copies.append(remote(gate_send.at[to], gate_recv.at[d], gate_sem, d, kv=to))
-        gate_copies[-1].start()
     win_k = remote(wk.at[pl.ds(tok, WINDOW), :], wk.at[pl.ds(0, WINDOW), :], win_sem, 0, ctx=right)
     win_v = remote(wv.at[pl.ds(tok, WINDOW), :], wv.at[pl.ds(0, WINDOW), :], win_sem, 1, ctx=right)
     win_k.start()
     win_v.start()
 
-    kv_f32[0, pl.ds(STRIDE, tok), :] = wk[pl.ds(WINDOW, tok), :].astype(F32)
-    kv_f32[1, pl.ds(STRIDE, tok), :] = wv[pl.ds(WINDOW, tok), :].astype(F32)
     rim_k.wait()
     rim_v.wait()
     kv_f32[0, :STRIDE, :] = rim[0].astype(F32)
     kv_f32[1, :STRIDE, :] = rim[1].astype(F32)
-    loads[6].wait()
+    loads[4].wait()
     nb = tok // STRIDE
     row = lax.broadcasted_iota(jnp.int32, (nb, hd), 0)
-    for s in range(2):
+    loads[2].wait()
+    loads[3].wait()
+
+    def squeeze(s, carry):
         flat = jnp.concatenate(
             [kv_f32[s, pl.ds(b, nb, stride=STRIDE), :] for b in range(BLOCK)], axis=1
         ).astype(BF16)
-        loads[4 + s].wait()
         hidden = jnp.dot(flat, one_v[s], preferred_element_type=F32)
         hidden = jax.nn.gelu(hidden).astype(BF16)
         packed = jnp.dot(hidden, two_v[s], preferred_element_type=F32)
         packed = jnp.where((row == 0) & (me == 0), 0.0, packed)
-        gath[s, y, z, core] = packed.astype(BF16)
-
-    k1 = [remote(gath.at[0, y, z, core], gath.at[0, y, z, core], y1_sem, d, ctx=y_peer(d)) for d in range(1, ny)]
-    v1 = [remote(gath.at[1, y, z, core], gath.at[1, y, z, core], z1_sem, d, ctx=z_peer(d)) for d in range(1, nz)]
+        gath[s, core, y, z] = packed.astype(BF16)
+        return carry
+
+    lax.fori_loop(0, 2, squeeze, 0)
+    k1 = [remote(gath.at[0, core, y, z], gath.at[0, core, y, z], y1_sem, d, ctx=y_peer(d)) for d in range(1, ny)]
+    v1 = [remote(gath.at[1, core, y, z], gath.at[1, core, y, z], z1_sem, d, ctx=z_peer(d)) for d in range(1, nz)]
     for c in k1 + v1:
         c.start()
 
-    nfull = (me * nb) // KC
-    ids = lax.broadcasted_iota(jnp.int32, (KC, tok), 0) + nfull * KC
-    at = lax.broadcasted_iota(jnp.int32, (KC, tok), 1) + tok * me
-    far_bias[...] = jnp.where((ids * STRIDE + STRIDE - 1 <= at) | (ids == 0), 0.0, NEG)
+    slot = y * nz + z
+    per = KC // nb
+    nfull = slot // per
+    for par in range(nc):
+        i = lax.broadcasted_iota(jnp.int32, (KC, tok), 0) + nfull * KC
+        ids = (i // nb) * (nc * nb) + par * nb + lax.rem(i, nb)
+        at = lax.broadcasted_iota(jnp.int32, (KC, tok), 1) + tok * me
+        far_bias[par] = jnp.where((ids * STRIDE + STRIDE - 1 <= at) | (ids == 0), 0.0, NEG)
     width = WINDOW + HALF
     for i in range(tok // HALF):
         w = lax.broadcasted_iota(jnp.int32, (width, HALF), 0)
@@ -153,20 +152,24 @@
     cvt[hd:, :] = one_row(cvt.shape[1])
     wvt[:hd, WINDOW:] = kv_f32[1, pl.ds(STRIDE, tok), :].T.astype(BF16)
 
-    logits = gate_send[group].astype(F32)
+    loads[6].wait()
+    loads[7].wait()
+    part = lax.dot_general(gw_v[...], inp_v[...], NT, preferred_element_type=F32)
+    gate_send[...] = part.astype(BF16).reshape(gate_send.shape)
+    gate_copies = []
     for d in range(1, nkv):
-        gate_copies[d - 1].wait()
-        logits = logits + gate_recv[d].astype(F32)
-    gates[...] = jax.nn.sigmoid(logits)
+        to = kv_peer(d)
+        gate_copies.append(remote(gate_send.at[to], gate_recv.at[d], gate_sem, d, kv=to))
+        gate_copies[-1].start()
 
     win_k.wait()
     win_v.wait()
     wvt[:hd, :WINDOW] = wv[:WINDOW, :].astype(F32).T.astype(BF16)
-    loads[7].wait()
-
-    k2 = [remote(gath.at[0, :, z, core], gath.at[0, :, z, core], z2_sem, d, ctx=z_peer(d)) for d in range(1, nz)]
-    v2 = [remote(gath.at[1, y, :, core], gath.at[1, y, :, core], y2_sem, d, ctx=y_peer(d)) for d in range(1, ny)]
-    swap = remote(gath.at[:, :, :, core], gath.at[:, :, :, core], core_sem, 0, ctx=partner)
+    loads[5].wait()
+
+    k2 = [remote(gath.at[0, core, :, z], gath.at[0, core, :, z], z2_sem, d, ctx=z_peer(d)) for d in range(1, nz)]
+    v2 = [remote(gath.at[1, core, y], gath.at[1, core, y], y2_sem, d, ctx=y_peer(d)) for d in range(1, ny)]
+    swap = remote(gath.at[:, core], gath.at[:, core], core_sem, 0, ctx=partner)
 
     def second():
         for c in k1 + v1:
@@ -202,84 +205,103 @@
         for i in range(tok // HALF):
             cols = slice(i * HALF, (i + 1) * HALF)
             o = jnp.dot(wvt[:, i * HALF : i * HALF + width], e[:, cols], preferred_element_type=F32)
-            near_ref[h, :, cols] = o[:hd] * (gates[pl.ds(heads + h, 1), cols] / o[hd : hd + 1])
+            near_ref[h, :, cols] = o[:hd] * (1.0 / o[hd : hd + 1])
 
     near_scores(0, s0, c0)
 
-    def near_pair(j, carry):
-        h = 2 * j
-        near_scores(h + 1, s1, c1)
-        near_values(h, s0, c0)
-        near_scores(jnp.minimum(h + 2, heads - 2), s0, c0)
-        near_values(h + 1, s1, c1)
+    def near_group(j, carry):
+        for u in range(0, UNROLL, 2):
+            h = UNROLL * j + u
+            near_scores(h + 1, s1, c1)
+            near_values(h, s0, c0)
+            near_scores(jnp.minimum(h + 2, heads - 2), s0, c0)
+            near_values(h + 1, s1, c1)
         pl.when(j == STEP2)(second)
-        pl.when(j == STEP3)(third)
         return carry
 
-    lax.fori_loop(0, heads // 2, near_pair, 0)
-
-    swap.wait()
-    per_y = nz * nc * nb
-    for i in range(ny):
-        vals = gath[1, i].reshape(per_y, hd)
-        cvt[:hd, i * per_y : (i + 1) * per_y] = vals.astype(F32).T.astype(BF16)
+    lax.fori_loop(0, heads // UNROLL, near_group, 0)
+
+    third()
+    logits = gate_send[group].astype(F32)
+    for d in range(1, nkv):
+        gate_copies[d - 1].wait()
+        logits = logits + gate_recv[d].astype(F32)
+    gates[...] = jax.nn.sigmoid(logits)
+
 
     m_ref[...] = jnp.zeros_like(m_ref)
     acc_ref[...] = jnp.zeros_like(acc_ref)
-
-    def far_scores(c, h, s_ref, c_ref, masked):
-        k = gath[0, c].reshape(KC, hd)
+    half = cvt.shape[1] // nc
+    keys_all = gath.reshape(2, nc, half, hd)
+
+    def far_scores(par, first, w, h, s_ref, c_ref, masked):
+        k = keys_all[0, par, pl.ds(first, w), :]
         s = lax.dot_general(k, q_v[:, head_cols(h)], NT, preferred_element_type=F32)
         if masked:
-            s = s + far_bias[...]
-        s_ref[:KC, :] = s
+            s = s + far_bias[par, :w, :]
+        s_ref[:w, :] = s
         c_ref[...] = fold(s)
 
-    def far_values(c, h, s_ref, c_ref):
+    def far_values(par, first, w, h, s_ref, c_ref, last):
         m_old = m_ref[pl.ds(h, 1), :]
         m = jnp.maximum(jnp.max(c_ref[...], axis=0, keepdims=True) * scale, m_old)
-        e = jnp.exp2(s_ref[:KC, :] * scale - m).astype(BF16)
-        vt = cvt[:, pl.ds(pl.multiple_of(c * KC, KC), KC)]
+        e = jnp.exp2(s_ref[:w, :] * scale - m).astype(BF16)
+        vt = cvt[:, pl.ds(pl.multiple_of(par * half + first, KC), w)]
         o = jnp.dot(vt, e, preferred_element_type=F32)
-        acc_ref[h] = acc_ref[h] * jnp.exp2(m_old - m) + o
-        m_ref[pl.ds(h, 1), :] = m
-
-    def far_sweep(chunk_of, head_of, count, masked):
-        far_scores(chunk_of(0), head_of(0), s0, c0, masked)
-
-        def pair(j, carry):
-            n = 2 * j
-            far_scores(chunk_of(n + 1), head_of(n + 1), s1, c1, masked)
-            far_values(chunk_of(n), head_of(n), s0, c0)
-            nxt = jnp.minimum(n + 2, count - 2)
-            far_scores(chunk_of(nxt), head_of(nxt), s0, c0, masked)
-            far_values(chunk_of(n + 1), head_of(n + 1), s1, c1)
-            return carry
-
-        lax.fori_loop(0, count // 2, pair, 0)
-
-    @pl.when(nfull > 0)
-    def _():
-        far_sweep(lambda n: n // heads, lambda n: lax.rem(n, heads), nfull * heads, False)
-
-    far_sweep(lambda n: nfull, lambda n: n, heads, True)
+        o = acc_ref[h] * jnp.exp2(m_old - m) + o
+        if last:
+            r = o[:hd] * (gates[pl.ds(h, 1), :] / o[hd : hd + 1]) + near_ref[h] * gates[pl.ds(heads + h, 1), :]
+            out_v[:, head_cols(h)] = r.T.astype(BF16)
+        else:
+            acc_ref[h] = o
+            m_ref[pl.ds(h, 1), :] = m
 
     def put(h):
         return pltpu.make_async_copy(out_v.at[:, head_cols(h)], out_hbm.at[:, head_cols(h)], out_sem.at[h])
 
-    def finish(h, carry):
-        o = acc_ref[h]
-        r = o[:hd] * (gates[pl.ds(h, 1), :] / o[hd : hd + 1]) + near_ref[h]
-        out_v[:, head_cols(h)] = r.T.astype(BF16)
-        put(h).start()
-        return carry
-
-    lax.fori_loop(0, heads, finish, 0)
+    def far_sweep(par, first, w, masked, last):
+        far_scores(par, first, w, 0, s0, c0, masked)
+
+        def group_of_heads(j, carry):
+            for u in range(0, UNROLL, 2):
+                h = UNROLL * j + u
+                far_scores(par, first, w, h + 1, s1, c1, masked)
+                far_values(par, first, w, h, s0, c0, last)
+                far_scores(par, first, w, jnp.minimum(h + 2, heads - 2), s0, c0, masked)
+                far_values(par, first, w, h + 1, s1, c1, last)
+            if last:
+                for u in range(UNROLL):
+                    put(UNROLL * j + u).start()
+            return carry
+
+        lax.fori_loop(0, heads // UNROLL, group_of_heads, 0)
+
+    for turn in range(nc):
+        par = core if turn == 0 else 1 - core
+        if turn:
+            swap.wait()
+        for i in range(ny):
+            vals = gath[1, par, i].reshape(nz * nb, hd)
+            cvt[:hd, pl.ds(pl.multiple_of(par * half + i * nz * nb, nz * nb), nz * nb)] = vals.astype(F32).T.astype(BF16)
+
+        def whole(i, carry):
+            far_sweep(par, pl.multiple_of(i * KC, KC), KC, False, False)
+            return carry
+
+        lax.fori_loop(0, nfull, whole, 0)
+        rest = lax.rem(slot, per) * nb // PIECE
+        for n in range(KC // PIECE):
+            @pl.when(rest == n)
+            def _():
+                far_sweep(par, pl.multiple_of(nfull * KC, KC), (n + 1) * PIECE, True, turn == nc - 1)
+
     for h in range(heads):
         put(h).wait()
 
 
-STEP2, STEP3 = 2, 6
+PIECE = 128
+STEP2 = 0
+UNROLL = 4
 
 
 def on_device(dims, queries, keys, values, inputs, gate_weight, comp_one, comp_two):
@@ -313,7 +335,7 @@
             vm((2, STRIDE, hd), BF16),
             vm((2, STRIDE + tok, hd), F32),
             vm((hd + 16, WINDOW + tok), BF16),
-            vm((2, ny, nz, nc, tok // STRIDE, hd), BF16),
+            vm((2, nc, ny, nz, tok // STRIDE, hd), BF16),
             vm((hd + 16, cols), BF16),
             vm((nkv, 2 * heads, tok), BF16),
             vm((nkv, 2 * heads, tok), BF16),
@@ -325,7 +347,7 @@
             vm((heads, tok), F32),
             vm((heads, hd + 16, tok), F32),
             vm((heads, hd, tok), F32),
-            vm((KC, tok), F32),
+            vm((nc, KC, tok), F32),
             vm((width, tok), F32),
             dma((8,)),
             dma((heads,)),

time: 56.3 us -> 50.9 us (0.904)
  Pallas kernels: 52.5 us -> 47.6 us
    pallas_call x1, Pallas kernels: 52.5 us -> 47.6 us  [on_device(): pl.pallas_call(functools.partial(kernel, dims), out_shape=jax.ShapeDtypeS...]
where the time goes in v2:
time: 50.9 us; the launch traced here: 50.8 us
  Pallas kernels  47.6 us (94%)
  local copies, waits for them, and re-layouts  3.16 us (6%)
    pallas_call x1, Pallas kernels, on_device(): pl.pallas_call(functools.partial(kernel, dims), out_shape=jax.ShapeDtypeS...  47.6 us
    unnamed x1, local copies, waits for them, and re-layouts  3.16 us

profile of v2, /device:TPU:24, one launch (start us, length us, event | category | flops | bytes accessed | tf_op | source)
XLA Modules:
  0.0 50.8 jit_solution(6708360986465097792)
XLA Ops:
  0.0 47.6 %attend.1 = bf16[512,2048]{1,0:T(8,128)(2,1)} custom-call(bf16[512,2048]{1,0:T(8,128)(2,1)} %bitcast.11, bf16[512,128]{1,0:T(8,128)(2,1)} %bitcast.13, bf16[512,128]{1,0:T(8,128)(2,1)} %bitcast.14, bf16[512,1152]{1,0:T(8,128)(2,1)} %inputs_hbm.1, bf16[128,1152]{1,0:T(8,128)(2,1)} %bitcast.12, bf16[2,4096,256]{2,1,0:T(8,128)(2,1)} %bitcast.10, ...), custom_call_target="tpu_custom_call" | custom-call | tf_op jit(solution)/shard_map/attend/pallas_call | solution.py:321
  47.6 3.2 %copy.9 = bf16[512,1,2048]{2,0,1:T(8,128)(2,1)} copy(bf16[512,1,2048]{2,0,1:T(8,128)(2,1)} %bitcast.9) | data formatting | bytes 4194304

commit v3 on v2

--- a/solution.py
+++ b/solution.py
@@ -23,11 +23,11 @@
 def kernel(
     dims,
     q_hbm, keys_hbm, values_hbm, inputs_hbm, gate_w_hbm, one_hbm, two_hbm,
-    out_hbm,
-    q_v, out_v, inp_v, gw_v, one_v, two_v,
+    out_v,
+    q_v, inp_v, gw_v, one_v, two_v,
     wk, wv, rim, kv_f32, wvt, gath, cvt, gate_send, gate_recv, gates,
     s0, s1, c0, c1, m_ref, acc_ref, near_ref, far_bias, near_bias,
-    in_sem, out_sem, rim_sem, win_sem, gate_sem, y1_sem, z1_sem, z2_sem, y2_sem, core_sem,
+    in_sem, rim_sem, win_sem, gate_sem, y1_sem, z1_sem, z2_sem, y2_sem, core_sem,
 ):
     ny, nz, nc, nkv, heads = dims
     n_ctx = ny * nz * nc
@@ -60,7 +60,7 @@
         load(inputs_hbm, inp_v, 5),
         load(gate_w_hbm, gw_v, 6),
     ]
-    for c in loads:
+    for c in loads[:5]:
         c.start()
 
     barrier = pltpu.get_barrier_semaphore()
@@ -110,6 +110,8 @@
     row = lax.broadcasted_iota(jnp.int32, (nb, hd), 0)
     loads[2].wait()
     loads[3].wait()
+    for c in loads[5:]:
+        c.start()
 
     def squeeze(s, carry):
         flat = jnp.concatenate(
@@ -152,6 +154,13 @@
     cvt[hd:, :] = one_row(cvt.shape[1])
     wvt[:hd, WINDOW:] = kv_f32[1, pl.ds(STRIDE, tok), :].T.astype(BF16)
 
+    m_ref[...] = jnp.zeros_like(m_ref)
+
+    def init(h, carry):
+        acc_ref[h] = jnp.zeros(acc_ref.shape[1:], F32)
+        return carry
+
+    lax.fori_loop(0, heads, init, 0)
     loads[6].wait()
     loads[7].wait()
     part = lax.dot_general(gw_v[...], inp_v[...], NT, preferred_element_type=F32)
@@ -229,8 +238,6 @@
     gates[...] = jax.nn.sigmoid(logits)
 
 
-    m_ref[...] = jnp.zeros_like(m_ref)
-    acc_ref[...] = jnp.zeros_like(acc_ref)
     half = cvt.shape[1] // nc
     keys_all = gath.reshape(2, nc, half, hd)
 
@@ -256,9 +263,6 @@
             acc_ref[h] = o
             m_ref[pl.ds(h, 1), :] = m
 
-    def put(h):
-        return pltpu.make_async_copy(out_v.at[:, head_cols(h)], out_hbm.at[:, head_cols(h)], out_sem.at[h])
-
     def far_sweep(par, first, w, masked, last):
         far_scores(par, first, w, 0, s0, c0, masked)
 
@@ -269,9 +273,6 @@
                 far_values(par, first, w, h, s0, c0, last)
                 far_scores(par, first, w, jnp.minimum(h + 2, heads - 2), s0, c0, masked)
                 far_values(par, first, w, h + 1, s1, c1, last)
-            if last:
-                for u in range(UNROLL):
-                    put(UNROLL * j + u).start()
             return carry
 
         lax.fori_loop(0, heads // UNROLL, group_of_heads, 0)
@@ -294,9 +295,6 @@
             @pl.when(rest == n)
             def _():
                 far_sweep(par, pl.multiple_of(nfull * KC, KC), (n + 1) * PIECE, True, turn == nc - 1)
-
-    for h in range(heads):
-        put(h).wait()
 
 
 PIECE = 128
@@ -321,10 +319,9 @@
     out = pl.pallas_call(
         functools.partial(kernel, dims),
         out_shape=jax.ShapeDtypeStruct((tok, heads * hd), BF16),
-        in_specs=[any_spec] * 7,
-        out_specs=any_spec,
+        in_specs=[pl.BlockSpec(memory_space=pltpu.HBM)] * 7,
+        out_specs=pl.BlockSpec(memory_space=pltpu.VMEM),
         scratch_shapes=[
-            vm((tok, heads * hd), BF16),
             vm((tok, heads * hd), BF16),
             vm((tok, depth), BF16),
             vm((gate_rows, depth), BF16),
@@ -350,7 +347,6 @@
             vm((nc, KC, tok), F32),
             vm((width, tok), F32),
             dma((8,)),
-            dma((heads,)),
             dma((2, 2)),
             dma((2, 2)),
             dma((2, nkv)),
@@ -361,10 +357,10 @@
             dma((2, 1)),
         ],
         compiler_params=pltpu.CompilerParams(
-            collective_id=0, has_side_effects=True, vmem_limit_bytes=58 * 1024 * 1024
+            collective_id=0, has_side_effects=True, vmem_limit_bytes=44 * 1024 * 1024
         ),
         name="attend",
-    )(
+    )(*[pltpu.with_memory_space_constraint(a, pltpu.HBM) for a in (
         q,
         keys.reshape(tok, hd),
         values.reshape(tok, hd),
@@ -372,7 +368,7 @@
         gate_w,
         comp_one.reshape(comp_one.shape[1:]),
         comp_two.reshape(comp_two.shape[1:]),
-    )
+    )])
     return out.reshape(tok, 1, heads * hd)
 
 

time: 50.9 us -> 47.7 us (0.937)
  local copies, waits for them, and re-layouts: 3.16 us -> 1.32 us
  Pallas kernels: 47.6 us -> 46.3 us
    unnamed x1, local copies, waits for them, and re-layouts: 3.16 us -> 1.32 us
    pallas_call x1, Pallas kernels: 47.6 us -> 46.3 us  [on_device(): pl.pallas_call(functools.partial(kernel, dims), out_shape=jax.ShapeDtypeS...]
where the time goes in v3:
time: 47.7 us; the launch traced here: 47.6 us
  Pallas kernels  46.3 us (97%)
  local copies, waits for them, and re-layouts  1.32 us (3%)
    pallas_call x1, Pallas kernels, on_device(): pl.pallas_call(functools.partial(kernel, dims), out_shape=jax.ShapeDtypeS...  46.3 us
    unnamed x1, local copies, waits for them, and re-layouts  1.32 us

profile of v3, /device:TPU:24, one launch (start us, length us, event | category | flops | bytes accessed | tf_op | source)
XLA Modules:
  0.0 47.6 jit_solution(16925953964560709325)
XLA Ops:
  0.0 46.3 %attend.1 = bf16[512,2048]{1,0:T(8,128)(2,1)S(1)} custom-call(bf16[512,2048]{1,0:T(8,128)(2,1)} %bitcast.11, bf16[512,128]{1,0:T(8,128)(2,1)} %bitcast.13, bf16[512,128]{1,0:T(8,128)(2,1)} %bitcast.14, bf16[512,1152]{1,0:T(8,128)(2,1)} %inputs_hbm.1, bf16[128,1152]{1,0:T(8,128)(2,1)} %bitcast.12, bf16[2,4096,256]{2,1,0:T(8,128)(2,1)} %bitcast.10, ...), custom_call_target="tpu_custom_call" | custom-call | tf_op jit(solution)/shard_map/attend/pallas_call | solution.py:319
  46.3 1.3 %copy.9 = bf16[512,1,2048]{2,0,1:T(8,128)(2,1)} copy(bf16[512,1,2048]{2,0,1:T(8,128)(2,1)S(1)} %bitcast.9) | data formatting | bytes 4194304

commit v4 on v3

--- a/solution.py
+++ b/solution.py
@@ -154,13 +154,6 @@
     cvt[hd:, :] = one_row(cvt.shape[1])
     wvt[:hd, WINDOW:] = kv_f32[1, pl.ds(STRIDE, tok), :].T.astype(BF16)
 
-    m_ref[...] = jnp.zeros_like(m_ref)
-
-    def init(h, carry):
-        acc_ref[h] = jnp.zeros(acc_ref.shape[1:], F32)
-        return carry
-
-    lax.fori_loop(0, heads, init, 0)
     loads[6].wait()
     loads[7].wait()
     part = lax.dot_general(gw_v[...], inp_v[...], NT, preferred_element_type=F32)
@@ -205,12 +198,12 @@
                 preferred_element_type=F32,
             )
             s = s + near_bias[:, cols]
-            s_ref[:, cols] = s
+            s_ref[:width, cols] = s
             c_ref[:, cols] = fold(s)
 
     def near_values(h, s_ref, c_ref):
         m = jnp.max(c_ref[...], axis=0, keepdims=True) * scale
-        e = jnp.exp2(s_ref[...] * scale - m).astype(BF16)
+        e = jnp.exp2(s_ref[:width, :] * scale - m).astype(BF16)
         for i in range(tok // HALF):
             cols = slice(i * HALF, (i + 1) * HALF)
             o = jnp.dot(wvt[:, i * HALF : i * HALF + width], e[:, cols], preferred_element_type=F32)
@@ -241,41 +234,48 @@
     half = cvt.shape[1] // nc
     keys_all = gath.reshape(2, nc, half, hd)
 
-    def far_scores(par, first, w, h, s_ref, c_ref, masked):
-        k = keys_all[0, par, pl.ds(first, w), :]
+    def far_scores(par, w, h, s_ref, c_ref):
+        k = keys_all[0, par, :w, :]
         s = lax.dot_general(k, q_v[:, head_cols(h)], NT, preferred_element_type=F32)
-        if masked:
-            s = s + far_bias[par, :w, :]
-        s_ref[:w, :] = s
-        c_ref[...] = fold(s)
-
-    def far_values(par, first, w, h, s_ref, c_ref, last):
-        m_old = m_ref[pl.ds(h, 1), :]
-        m = jnp.maximum(jnp.max(c_ref[...], axis=0, keepdims=True) * scale, m_old)
+        free = (w - 1) // KC * KC
+        end = s[free:] + far_bias[par, : w - free, :]
+        top = fold(end)
+        if free:
+            s_ref[:free, :] = s[:free]
+            top = jnp.maximum(top, fold(s[:free]))
+        s_ref[free:w, :] = end
+        c_ref[...] = top
+
+    def far_values(par, w, h, s_ref, c_ref, last):
+        m = jnp.maximum(jnp.max(c_ref[...], axis=0, keepdims=True) * scale, 0.0)
+        if last:
+            m_old = m_ref[pl.ds(h, 1), :]
+            m = jnp.maximum(m, m_old)
         e = jnp.exp2(s_ref[:w, :] * scale - m).astype(BF16)
-        vt = cvt[:, pl.ds(pl.multiple_of(par * half + first, KC), w)]
+        vt = cvt[:, pl.ds(pl.multiple_of(par * half, half), w)]
         o = jnp.dot(vt, e, preferred_element_type=F32)
-        o = acc_ref[h] * jnp.exp2(m_old - m) + o
         if last:
+            o = acc_ref[h] * jnp.exp2(m_old - m) + o
             r = o[:hd] * (gates[pl.ds(h, 1), :] / o[hd : hd + 1]) + near_ref[h] * gates[pl.ds(heads + h, 1), :]
             out_v[:, head_cols(h)] = r.T.astype(BF16)
         else:
             acc_ref[h] = o
             m_ref[pl.ds(h, 1), :] = m
 
-    def far_sweep(par, first, w, masked, last):
-        far_scores(par, first, w, 0, s0, c0, masked)
+    def far_sweep(par, w, last):
+        unroll = UNROLL if w <= KC else WIDE
+        far_scores(par, w, 0, s0, c0)
 
         def group_of_heads(j, carry):
-            for u in range(0, UNROLL, 2):
-                h = UNROLL * j + u
-                far_scores(par, first, w, h + 1, s1, c1, masked)
-                far_values(par, first, w, h, s0, c0, last)
-                far_scores(par, first, w, jnp.minimum(h + 2, heads - 2), s0, c0, masked)
-                far_values(par, first, w, h + 1, s1, c1, last)
+            for u in range(0, unroll, 2):
+                h = unroll * j + u
+                far_scores(par, w, h + 1, s1, c1)
+                far_values(par, w, h, s0, c0, last)
+                far_scores(par, w, jnp.minimum(h + 2, heads - 2), s0, c0)
+                far_values(par, w, h + 1, s1, c1, last)
             return carry
 
-        lax.fori_loop(0, heads // UNROLL, group_of_heads, 0)
+        lax.fori_loop(0, heads // unroll, group_of_heads, 0)
 
     for turn in range(nc):
         par = core if turn == 0 else 1 - core
@@ -285,19 +285,18 @@
             vals = gath[1, par, i].reshape(nz * nb, hd)
             cvt[:hd, pl.ds(pl.multiple_of(par * half + i * nz * nb, nz * nb), nz * nb)] = vals.astype(F32).T.astype(BF16)
 
-        def whole(i, carry):
-            far_sweep(par, pl.multiple_of(i * KC, KC), KC, False, False)
-            return carry
-
-        lax.fori_loop(0, nfull, whole, 0)
-        rest = lax.rem(slot, per) * nb // PIECE
-        for n in range(KC // PIECE):
-            @pl.when(rest == n)
+        need = (slot + 1) * nb
+        lower = 0
+        for w in WIDTHS:
+            @pl.when((need > lower) & (need <= w))
             def _():
-                far_sweep(par, pl.multiple_of(nfull * KC, KC), (n + 1) * PIECE, True, turn == nc - 1)
-
-
-PIECE = 128
+                far_sweep(par, w, turn == nc - 1)
+
+            lower = w
+
+
+WIDTHS = (512, 768, 896, 1024)
+WIDE = 4
 STEP2 = 0
 UNROLL = 4
 
@@ -337,8 +336,8 @@
             vm((nkv, 2 * heads, tok), BF16),
             vm((nkv, 2 * heads, tok), BF16),
             vm((2 * heads, tok), F32),
-            vm((width, tok), F32),
-            vm((width, tok), F32),
+            vm((cols // nc, tok), F32),
+            vm((cols // nc, tok), F32),
             vm((8, tok), F32),
             vm((8, tok), F32),
             vm((heads, tok), F32),

time: 47.7 us -> 45.5 us (0.954)
  Pallas kernels: 46.3 us -> 44.1 us
    pallas_call x1, Pallas kernels: 46.3 us -> 44.1 us  [on_device(): pl.pallas_call(functools.partial(kernel, dims), out_shape=jax.ShapeDtypeS...]
where the time goes in v4:
time: 45.5 us
  Pallas kernels  44.1 us (97%)
  local copies, waits for them, and re-layouts  1.32 us (3%)
    pallas_call x1, Pallas kernels, on_device(): pl.pallas_call(functools.partial(kernel, dims), out_shape=jax.ShapeDtypeS...  44.1 us
    unnamed x1, local copies, waits for them, and re-layouts  1.32 us

profile of v4, /device:TPU:24, one launch (start us, length us, event | category | flops | bytes accessed | tf_op | source)
XLA Modules:
  0.0 45.5 jit_solution(12512644711410477107)
XLA Ops:
  0.0 44.1 %attend.1 = bf16[512,2048]{1,0:T(8,128)(2,1)S(1)} custom-call(bf16[512,2048]{1,0:T(8,128)(2,1)} %bitcast.11, bf16[512,128]{1,0:T(8,128)(2,1)} %bitcast.13, bf16[512,128]{1,0:T(8,128)(2,1)} %bitcast.14, bf16[512,1152]{1,0:T(8,128)(2,1)} %inputs_hbm.1, bf16[128,1152]{1,0:T(8,128)(2,1)} %bitcast.12, bf16[2,4096,256]{2,1,0:T(8,128)(2,1)} %bitcast.10, ...), custom_call_target="tpu_custom_call" | custom-call | tf_op jit(solution)/shard_map/attend/pallas_call | solution.py:318
  44.2 1.3 %copy.9 = bf16[512,1,2048]{2,0,1:T(8,128)(2,1)} copy(bf16[512,1,2048]{2,0,1:T(8,128)(2,1)S(1)} %bitcast.9) | data formatting | bytes 4194304

commit v5 on v4

--- a/solution.py
+++ b/solution.py
@@ -224,13 +224,6 @@
     lax.fori_loop(0, heads // UNROLL, near_group, 0)
 
     third()
-    logits = gate_send[group].astype(F32)
-    for d in range(1, nkv):
-        gate_copies[d - 1].wait()
-        logits = logits + gate_recv[d].astype(F32)
-    gates[...] = jax.nn.sigmoid(logits)
-
-
     half = cvt.shape[1] // nc
     keys_all = gath.reshape(2, nc, half, hd)
 
@@ -281,6 +274,11 @@
         par = core if turn == 0 else 1 - core
         if turn:
             swap.wait()
+            logits = gate_send[group].astype(F32)
+            for d in range(1, nkv):
+                gate_copies[d - 1].wait()
+                logits = logits + gate_recv[d].astype(F32)
+            gates[...] = jax.nn.sigmoid(logits)
         for i in range(ny):
             vals = gath[1, par, i].reshape(nz * nb, hd)
             cvt[:hd, pl.ds(pl.multiple_of(par * half + i * nz * nb, nz * nb), nz * nb)] = vals.astype(F32).T.astype(BF16)

time: 45.5 us -> 45.6 us (level)
  no operation moved by 1% of the time
where the time goes in v5:
time: 45.6 us; the launch traced here: 45.5 us
  Pallas kernels  44.2 us (97%)
  local copies, waits for them, and re-layouts  1.32 us (3%)
    pallas_call x1, Pallas kernels, on_device(): pl.pallas_call(functools.partial(kernel, dims), out_shape=jax.ShapeDtypeS...  44.2 us
    unnamed x1, local copies, waits for them, and re-layouts  1.32 us

profile of v5, /device:TPU:24, one launch (start us, length us, event | category | flops | bytes accessed | tf_op | source)
XLA Modules:
  0.0 45.5 jit_solution(1241660227685170557)
XLA Ops:
  0.0 44.2 %attend.1 = bf16[512,2048]{1,0:T(8,128)(2,1)S(1)} custom-call(bf16[512,2048]{1,0:T(8,128)(2,1)} %bitcast.11, bf16[512,128]{1,0:T(8,128)(2,1)} %bitcast.13, bf16[512,128]{1,0:T(8,128)(2,1)} %bitcast.14, bf16[512,1152]{1,0:T(8,128)(2,1)} %inputs_hbm.1, bf16[128,1152]{1,0:T(8,128)(2,1)} %bitcast.12, bf16[2,4096,256]{2,1,0:T(8,128)(2,1)} %bitcast.10, ...), custom_call_target="tpu_custom_call" | custom-call | tf_op jit(solution)/shard_map/attend/pallas_call | solution.py:316
  44.2 1.3 %copy.9 = bf16[512,1,2048]{2,0,1:T(8,128)(2,1)} copy(bf16[512,1,2048]{2,0,1:T(8,128)(2,1)S(1)} %bitcast.9) | data formatting | bytes 4194304
